TPU v7x, 32 devices: a whole 2x2x4 slice. The times are simulated.
32 devices in a mesh: row: 8 (over y, x, core), col: 4 (over z).
Axes of the slice: x: 2, y: 2, z: 4, core: 2. Of those that a mesh axis runs over, the one named last changes fastest.
Arguments:
- image: bfloat16 [512, 512, 512], P('row', 'col'), may hold values from -6 to 6
- w_local: bfloat16 [3, 3, 512, 128], replicated, may hold values from -0.09375 to 0.09375
- w_cross: bfloat16 [3, 3, 128, 384], replicated, may hold values from -0.1875 to 0.1875
- w_spec: bfloat16 [768, 768], replicated, may hold values from -0.21875 to 0.21875
Outputs:
- result: bfloat16 [512, 512, 512], P('row', 'col')
All inputs are finite; a program needn't handle non-finite values.
Results may differ from a plain program's by a relative error of at most 0.0055.
Values may be sent and summed in bfloat16 or wider, within the bound.
A program may use at most 192 MiB of HBM per device.

v0:
```python
import jax
import jax.numpy as jnp
import numpy as np
from jax import lax
from jax.sharding import PartitionSpec as P

BOTH = ("row", "col")


def rounded(table):
    return np.asarray(table, np.float32).astype(jnp.bfloat16)


def column_table(height):
    freq = np.arange(height // 2)
    angle = 2.0 * np.pi * (np.outer(freq, np.arange(height)) % height) / height
    table = np.stack([np.cos(angle), -np.sin(angle)], axis=1)
    table[0, 1] = 1.0 - 2.0 * (np.arange(height) % 2)
    return rounded(table.reshape(height, height) / np.sqrt(height))


def width_order(nrow, ncol, width):
    part = width // (nrow * ncol)
    r, c, i = np.meshgrid(np.arange(nrow), np.arange(ncol), np.arange(part), indexing="ij")
    return (c * (width // ncol) + r * part + i).reshape(-1)


def width_tables(order, width, padded):
    half = width // 2
    count = width + 2
    plain = np.concatenate([np.arange(width), [0, half]])
    packed = np.concatenate([np.arange(half + 1), np.arange(half + 1)])
    rows = np.arange(count)
    out = []
    for freq in (plain, packed):
        angle = 2.0 * np.pi * (np.outer(freq, order) % width) / width
        pair = np.zeros((2, padded, width))
        pair[0, :count] = np.cos(angle) / np.sqrt(width)
        pair[1, :count] = np.sin(angle) / np.sqrt(width)
        out.append(rounded(pair))
    sign = np.where(rows <= half, 1.0, -1.0)
    scale_plain = np.where(np.isin(rows, [0, half, width, width + 1]), 1.0, 2.0)
    scale_packed = np.where(np.isin(packed, [0, half]), 1.0, 2.0)
    extra = padded - count
    pad = lambda v: np.pad(v, (0, extra))
    upper = pad((rows <= half).astype(np.float64))
    lower = pad((rows > half).astype(np.float64))
    return (out[0], out[1], pad(sign), upper, lower, pad(scale_plain), pad(scale_packed))


def assembled(pair, blocks, xp):
    cosine, sine = (pair[0], pair[1])
    pick = {"c": cosine, "s": sine}
    lines = []
    for line in blocks:
        lines.append(xp.concatenate([pick[k] * v[:, None] for k, v in line], axis=1))
    return xp.concatenate(lines, axis=0)


def extended(cells, sides, width):
    for axis, dim in sides:
        count = lax.axis_size(axis)
        ends = count - 1
        head = lax.slice_in_dim(cells, 0, width, axis=dim)
        tail = lax.slice_in_dim(cells, cells.shape[dim] - width, cells.shape[dim], axis=dim)
        cells = jnp.concatenate(
            [
                lax.ppermute(tail, axis, [(i, (i + 1) % count) for i in range(ends)]),
                cells,
                lax.ppermute(head, axis, [((i + 1) % count, i) for i in range(ends)]),
            ],
            axis=dim,
        )
    return cells


def conv(padded, weight):
    return lax.conv_general_dilated(
        padded[None],
        weight,
        (1, 1),
        "VALID",
        dimension_numbers=("NHWC", "HWIO", "NHWC"),
        preferred_element_type=jnp.float32,
    )[0]


def product(form, left, right):
    return jnp.einsum(form, left, right, preferred_element_type=jnp.float32)


def global_branch(glob, w_spec):
    nrow, ncol = (lax.axis_size("row"), lax.axis_size("col"))
    count = nrow * ncol
    height, width, ch = (glob.shape[0] * nrow, glob.shape[1] * ncol, glob.shape[2])
    bins = height // (2 * count)
    padded = -(-(width + 2) // 16) * 16
    columns = lax.all_to_all(glob, "row", split_axis=1, concat_axis=0, tiled=True)
    col_np = column_table(height)
    plain_np, packed_np, sign, upper, lower, scale_plain, scale_packed = width_tables(
        width_order(nrow, ncol, width), width, padded
    )
    ones = np.ones_like(sign)
    plain_form = ((("c", ones), ("s", ones)), (("s", -sign), ("c", sign)))
    packed_form = ((("c", upper), ("c", lower)), (("s", -upper), ("s", -lower)))

    def row_sums(pair, form, scale):
        table = assembled(pair.astype(np.float64), form, np) * np.tile(scale, 2)[:, None]
        return np.stack([table[:padded].sum(0), table[padded:].sum(0)], axis=1).astype(np.float32)

    def cast_form(form):
        return [[(k, jnp.asarray(rounded(v))) for k, v in line] for line in form]

    col_table = jnp.asarray(col_np)
    is_first = lax.axis_index(BOTH) == 0
    special = (is_first & (jnp.arange(bins) == 0))[:, None, None]
    table = jnp.where(
        special,
        assembled(jnp.asarray(packed_np), cast_form(packed_form), jnp)[None],
        assembled(jnp.asarray(plain_np), cast_form(plain_form), jnp)[None],
    )
    scale = jnp.where(
        special,
        jnp.asarray(scale_packed, jnp.float32)[None, :, None],
        jnp.asarray(scale_plain, jnp.float32)[None, :, None],
    )
    sums = jnp.where(
        special,
        jnp.asarray(row_sums(packed_np, packed_form, scale_packed))[None],
        jnp.asarray(row_sums(plain_np, plain_form, scale_plain))[None],
    )
    field = product("uh,hwc->uwc", col_table, columns).astype(jnp.bfloat16)
    lines = lax.all_to_all(field, BOTH, split_axis=0, concat_axis=1, tiled=True)
    lines = lines.reshape(bins, 2 * width, ch)
    spectrum = product("bmk,bkc->bmc", table, lines).astype(jnp.bfloat16)
    stacked = jnp.concatenate([spectrum[:, :padded], spectrum[:, padded:]], axis=-1)
    mixed = jnp.maximum(product("bvc,co->bvo", stacked, w_spec), 0.0)
    own_sum = jnp.sum(mixed, axis=(0, 1))
    every = lax.all_to_all(
        jnp.broadcast_to(own_sum[None], (count, 2 * ch)),
        BOTH,
        split_axis=0,
        concat_axis=0,
        tiled=True,
    )
    mean = jnp.sum(every, axis=0) / (height * (width // 2 + 1))
    scaled = (mixed * scale).astype(jnp.bfloat16)
    scaled = jnp.concatenate([scaled[..., :ch], scaled[..., ch:]], axis=1)
    offset = sums[:, :, :1] * mean[:ch] + sums[:, :, 1:] * mean[ch:]
    inverted = (product("bkm,bkc->bmc", table, scaled) - offset).astype(jnp.bfloat16)
    inverted = inverted.reshape(2 * bins, width, ch)
    back = lax.all_to_all(inverted, BOTH, split_axis=1, concat_axis=0, tiled=True)
    rows = product("uh,uwc->hwc", col_table, back).astype(jnp.bfloat16)
    return lax.all_to_all(rows, "row", split_axis=0, concat_axis=1, tiled=True)


def body(image, w_local, w_cross, w_spec):
    local_chan = w_cross.shape[2]
    spectral = global_branch(image[..., local_chan:], w_spec)
    padded = extended(image, (("row", 0), ("col", 1)), 1)
    local_out = conv(padded, w_local)
    cross_out = conv(padded[..., :local_chan], w_cross)
    result = jnp.concatenate(
        [local_out.astype(jnp.bfloat16), (cross_out + spectral).astype(jnp.bfloat16)], axis=-1
    )
    return result


def solution(mesh):
    in_specs = (P("row", "col", None), P(), P(), P())
    out_specs = P("row", "col", None)
    return jax.shard_map(body, mesh=mesh, in_specs=in_specs, out_specs=out_specs, check_vma=False)
```

profile of v0, /device:TPU:11, one launch (start us, length us, event | category | flops | bytes accessed | tf_op | source)
XLA Modules:
  0.0 627.0 jit_solution(2966774456978388852)
XLA Ops:
  0.0 11.6 %copy.97 = bf16[64,128,512]{2,0,1:T(8,128)(2,1)} copy(bf16[64,128,512]{2,1,0:T(8,128)(2,1)} %param.19) | data formatting | bytes 16777216 | tf_op args[0]
  14.4 74.4 %all_to_all.66 = bf16[64,128,384]{2,0,1:T(8,128)(2,1)S(1)} all-to-all(bf16[64,128,384]{2,0,1:T(8,128)(2,1)S(1)} %slice-done), channel_id=1, replica_groups=mesh['row'=8,'col'=4] {'row'}, dimensions={1} | all-to-all | bytes 12582912 | tf_op jit(solution)/shard_map/all_to_all | solution.py:98
  92.6 4.2 fusion.40
  96.8 6.4 %copy.108 = bf16[512,16,384]{2,1,0:T(8,128)(2,1)} copy(bf16[512,16,384]{2,0,1:T(8,128)(2,1)S(1)} %fusion.40) | data formatting | bytes 12582912 | tf_op jit(solution)/shard_map/convert_element_type | solution.py:132
  103.2 5.9 all-to-all-start.1
  109.3 137.3 %all-to-all-done.1 = bf16[512,16,384]{2,1,0:T(8,128)(2,1)} async-done(((bf16[512,16,384]{2,1,0:T(8,128)(2,1)}), bf16[512,16,384]{2,1,0:T(8,128)(2,1)}, u32[]{:S(2)}, u32[]{:S(2)}) %all-to-all-start.1) | async-done | bytes 6291488 | tf_op jit(solution)/shard_map/all_to_all | solution.py:133
  250.5 9.8 %fusion.20 = bf16[8,1056,384]{2,1,0:T(8,128)(2,1)S(1)} fusion(bf16[8,1024,384]{2,1,0:T(8,128)(2,1)S(1)} %bitcast.62, pred[8]{0:T(512)(128)(4,1)S(1)} %compare_and_fusion, bf16[1056,1024]{1,0:T(8,128)(2,1)S(1)} %copy-done.9, bf16[1056,1024]{1,0:T(8,128)(2,1)S(1)} %copy-done.10), kind=kOutput, calls=%fused_computation.28 | convolution fusion | flops 6655672320 | bytes 17104904 | tf_op jit(solution)/shard_map/bmk,bkc->bmc/dot_general | solution.py:89
  261.0 7.1 %maximum_reduce_fusion = (f32[768]{0:T(1024)S(1)}, bf16[8,528,768]{2,1,0:T(8,128)(2,1)}) fusion(f32[8,528]{1,0:T(8,128)S(1)} %broadcast_select_fusion.1, bf16[768,768]{1,0:T(8,128)(2,1)S(1)} %copy-done, bf16[8,528,384]{2,1,0:T(8,128)(2,1)S(1)} %get-tuple-element.14, bf16[8,528,384]{2,1,0:T(8,128)(2,1)S(1)} %get-tuple-element.13), kind=kOutput, calls=%fused_computation.14 | convolution fusion | flops 5008784384 | bytes 14175744 | tf_op jit(solution)/shard_map/bvc,co->bvo/dot_general | solution.py:89
  268.8 6.8 %all-to-all-start.2 = ((f32[32,1,768]{2,1,0:T(1,128)}), f32[32,1,768]{2,1,0:T(1,128)S(1)}, u32[]{:S(2)}, u32[]{:S(2)}) async-start(f32[32,1,768]{2,1,0:T(1,128)} %broadcast_in_dim.112), calls=%async_computation.2 | async-start | bytes 196608 | tf_op jit(solution)/shard_map/all_to_all | solution.py:139
  275.6 6.3 %fusion.64 = (bf16[8,528,384]{2,1,0:T(8,128)(2,1)}, bf16[8,528,384]{2,1,0:T(8,128)(2,1)}) fusion(bf16[8,528,768]{2,1,0:T(8,128)(2,1)} %get-tuple-element.6), kind=kLoop, calls=%fused_computation.73 | loop fusion | bytes 12976128 | tf_op jit(solution)/shard_map/slice | solution.py:148
  282.0 14.6 %subtract_convert_fusion = bf16[8,1024,384]{2,1,0:T(8,128)(2,1)S(1)} fusion(bf16[8,528,384]{2,1,0:T(8,128)(2,1)} %get-tuple-element.12, bf16[8,528,384]{2,1,0:T(8,128)(2,1)} %get-tuple-element.11, pred[8]{0:T(512)(128)(4,1)S(1)} %compare_and_fusion, bf16[1056,1024]{1,0:T(8,128)(2,1)S(1)} %copy-done.9, bf16[1056,1024]{1,0:T(8,128)(2,1)} %constant.82, ...), kind=kOutput, calls=%fused_computation.13 | convolution fusion | flops 6681133056 | bytes 17173512 | tf_op jit(solution)/shard_map/bkm,bkc->bmc/dot_general | solution.py:89
  296.6 6.4 %copy.111 = bf16[16,512,384]{2,0,1:T(8,128)(2,1)} copy(bf16[16,512,384]{2,1,0:T(8,128)(2,1)S(1)} %bitcast.59) | data formatting | bytes 12582912 | tf_op jit(solution)/shard_map/reshape | solution.py:151
  303.0 5.9 all-to-all-start.3
  315.2 36.4 %collective-permute-done = bf16[1,128,512]{2,1,0:T(8,128)(2,1)S(1)} collective-permute-done((bf16[1,128,512]{2,1,0:T(8,128)(2,1)S(1)}, bf16[1,128,512]{2,1,0:T(8,128)(2,1)S(1)}, u32[]{:S(2)}, u32[]{:S(2)}) %collective-permute-start) | collective-permute-done | bytes 131104 | tf_op jit(solution)/shard_map/ppermute | solution.py:68
  354.9 8.7 %collective-permute-start.3 = (bf16[66,1,512]{2,0,1:T(8,128)(2,1)S(1)}, bf16[66,1,512]{2,0,1:T(8,128)(2,1)S(1)}, u32[]{:S(2)}, u32[]{:S(2)}) collective-permute-start(bf16[66,1,512]{2,0,1:T(8,128)(2,1)S(1)} %get-tuple-element.8), channel_id=1, source_target_pairs={{1,0},{2,1},{3,2},{5,4},{6,5},{7,6},{9,8},{10,9},{11,10},{13,12},{... | collective-permute-start | bytes 202760 | tf_op jit(solution)/shard_map/ppermute | solution.py:70
  363.6 82.0 %collective-permute-done.2 = bf16[66,1,512]{2,0,1:T(8,128)(2,1)S(1)} collective-permute-done((bf16[66,1,512]{2,0,1:T(8,128)(2,1)S(1)}, bf16[66,1,512]{2,0,1:T(8,128)(2,1)S(1)}, u32[]{:S(2)}, u32[]{:S(2)}) %collective-permute-start.2) | collective-permute-done | bytes 67616 | tf_op jit(solution)/shard_map/ppermute | solution.py:68
  447.6 11.5 %fusion.72 = bf16[66,1,130,512]{3,0,2,1:T(8,128)(2,1)} fusion(bf16[66,1,512]{2,0,1:T(8,128)(2,1)S(1)} %collective-permute-done.3, bf16[1,128,512]{2,0,1:T(2,128)(2,1)S(1)} %copy.98, bf16[64,128,512]{2,0,1:T(8,128)(2,1)} %copy.97, bf16[1,128,512]{2,0,1:T(2,128)(2,1)S(1)} %copy.96, bf16[66,1,512]{2,0,1:T(8,128)(2,1)S(1)} %collective-permute-done.2), kind=kLoop, calls=%fused_computation.76 | loop fusion | flops 43929600 | bytes 17571840 | tf_op jit(solution)/shard_map/broadcast_in_dim | solution.py:79
  459.0 4.4 copy.112
  463.4 6.0 convert_bitcast_fusion.1
  469.4 9.1 %copy.114 = bf16[512,16,384]{2,1,0:T(8,128)(2,1)} copy(bf16[512,16,384]{0,2,1:T(8,128)(2,1)} %convert_bitcast_fusion.1) | data formatting | bytes 12582912 | tf_op jit(solution)/shard_map/convert_element_type | solution.py:153
  478.5 8.6 %all-to-all-start.4 = ((bf16[512,16,384]{2,1,0:T(8,128)(2,1)}), bf16[512,16,384]{2,1,0:T(8,128)(2,1)}, u32[]{:S(2)}, u32[]{:S(2)}) async-start(bf16[512,16,384]{2,1,0:T(8,128)(2,1)} %copy.114), calls=%async_computation.4 | async-start | bytes 12582912 | tf_op jit(solution)/shard_map/all_to_all | solution.py:154
  487.1 11.5 %pad_maximum_fusion = bf16[66,130,512]{2,0,1:T(8,128)(2,1)} fusion(bf16[66,1,512]{2,0,1:T(8,128)(2,1)S(1)} %collective-permute-done.3, bf16[1,128,512]{2,0,1:T(2,128)(2,1)S(1)} %copy.98, bf16[64,128,512]{2,0,1:T(8,128)(2,1)} %copy.97, bf16[1,128,512]{2,0,1:T(2,128)(2,1)S(1)} %copy.96, bf16[66,1,512]{2,0,1:T(8,128)(2,1)S(1)} %collective-permute-done.2), kind=kLoop, calls=%fused_computation.21 | loop fusion | flops 43929600 | bytes 17571840 | tf_op jit(solution)/shard_map/concatenate | solution.py:66
  498.6 8.2 %pad = bf16[66,1,136,512]{3,0,2,1:T(8,128)(2,1)} pad(bf16[66,1,130,512]{3,0,2,1:T(8,128)(2,1)} %fusion.72, bf16[]{:T(256)} %constant.62), padding=0_0x0_0x0_6x0_0 | pad | bytes 17977346 | tf_op jit(solution)/shard_map/broadcast_in_dim | solution.py:79
  506.7 10.6 %copy.100 = bf16[66,1,8,17,512]{4,2,3,0,1:T(8,128)(2,1)} copy(bf16[66,1,8,17,512]{4,0,3,2,1:T(8,128)(2,1)} %bitcast.56) | data formatting | bytes 18382848 | tf_op jit(solution)/shard_map/conv_general_dilated | solution.py:78
  522.2 21.4 %select_convert_fusion = bf16[64,8,17,128]{3,1,2,0:T(8,128)(2,1)S(1)} fusion(pred[8,17]{0,1:T(8,128)(4,1)S(1)} %copy-done.13, bf16[3,3,512,128]{3,2,1,0:T(8,128)(2,1)S(1)} %copy-done.8, bf16[66,1,7,2,512]{4,2,3,0,1:T(8,128)(2,1)S(1)} %slice.76, bf16[66,1,8,17,512]{4,2,3,0,1:T(8,128)(2,1)S(1)} %copy-done.2), kind=kOutput, calls=%fused_computation.44 | convolution fusion | flops 10300702720 | bytes 13545608 | tf_op jit(solution)/shard_map/conv_general_dilated | solution.py:78
  544.2 15.8 %convolution_select_fusion = f32[64,8,17,384]{3,1,2,0:T(8,128)} fusion(bf16[3,3,128,384]{3,2,1,0:T(8,128)(2,1)} %param.21, pred[8,17]{0,1:T(8,128)(4,1)S(1)} %copy-done.13, bf16[66,1,7,2,128]{4,2,3,0,1:T(8,128)(2,1)S(1)} %slice.79, bf16[66,1,8,17,128]{4,2,3,0,1:T(8,128)(2,1)S(1)} %copy.103), kind=kOutput, calls=%fused_computation.22 | convolution fusion | flops 7711789056 | bytes 16788616 | tf_op jit(solution)/shard_map/conv_general_dilated | solution.py:78
  560.0 12.2 %copy.104 = f32[64,8,17,384]{3,0,2,1:T(8,128)} copy(f32[64,8,17,384]{3,1,2,0:T(8,128)} %convolution_select_fusion) | data formatting | bytes 26738688 | tf_op jit(solution)/shard_map/conv_general_dilated | solution.py:78
  573.7 8.4 %convert_bitcast_fusion = f32[64,8,16,384]{3,2,0,1:T(8,128)} fusion(bf16[8,64,16,384]{3,2,1,0:T(8,128)(2,1)} %bitcast.26), kind=kLoop, calls=%fused_computation.12 | loop fusion | flops 3145728 | bytes 18874368 | tf_op jit(solution)/shard_map/convert_element_type | solution.py:164
  582.1 12.8 %copy.115 = f32[64,8,16,384]{3,0,2,1:T(8,128)} copy(f32[64,8,16,384]{3,2,0,1:T(8,128)} %convert_bitcast_fusion) | data formatting | bytes 25165824 | tf_op jit(solution)/shard_map/convert_element_type | solution.py:164
  594.9 12.6 %fusion.8 = bf16[64,128,384]{2,0,1:T(8,128)(2,1)} fusion(f32[64,1,136,384]{3,0,2,1:T(8,128)} %bitcast.55, f32[64,8,16,384]{3,0,2,1:T(8,128)} %copy.115), kind=kLoop, calls=%fused_computation.11 | loop fusion | flops 6291456 | bytes 31457280 | tf_op jit(solution)/shard_map/convert_element_type | solution.py:164
  607.5 7.8 %pad_maximum_fusion.1 = bf16[64,128,512]{2,0,1:T(8,128)(2,1)} fusion(bf16[64,128,384]{2,0,1:T(8,128)(2,1)} %fusion.8, bf16[64,128,128]{2,0,1:T(8,128)(2,1)S(1)} %copy-done.3), kind=kLoop, calls=%fused_computation.27 | loop fusion | flops 16777216 | bytes 16777216 | tf_op jit(solution)/shard_map/concatenate | solution.py:163
  615.3 11.5 %copy.116 = bf16[64,128,512]{2,1,0:T(8,128)(2,1)} copy(bf16[64,128,512]{2,0,1:T(8,128)(2,1)} %pad_maximum_fusion.1) | data formatting | bytes 16777216 | tf_op jit(solution)/shard_map/concatenate | solution.py:163
  (60 shorter events, 30.5 us)
Async XLA Ops:
  0.0 261.0 %copy-start = (bf16[768,768]{1,0:T(8,128)(2,1)S(1)}, bf16[768,768]{1,0:T(8,128)(2,1)}, u32[]{:S(2)}) copy-start(bf16[768,768]{1,0:T(8,128)(2,1)} %param.22) | copy-start | bytes 3538948
  11.6 2.8 slice-start
  88.8 3.8 copy-start.12
  103.2 5.9 copy-start.6
  103.2 5.9 copy-start.7
  103.2 6.0 copy-start.4
  103.2 6.0 copy-start.5
  103.2 143.4 %all-to-all-start.1 = ((bf16[512,16,384]{2,1,0:T(8,128)(2,1)}), bf16[512,16,384]{2,1,0:T(8,128)(2,1)}, u32[]{:S(2)}, u32[]{:S(2)}) async-start(bf16[512,16,384]{2,1,0:T(8,128)(2,1)} %copy.108), calls=%async_computation.1 | async-start | bytes 12582912 | tf_op jit(solution)/shard_map/all_to_all | solution.py:133
  109.1 141.4 %copy-start.9 = (bf16[1056,1024]{1,0:T(8,128)(2,1)S(1)}, bf16[1056,1024]{1,0:T(8,128)(2,1)}, u32[]{:S(2)}) copy-start(bf16[1056,1024]{1,0:T(8,128)(2,1)} %constant.91) | copy-start | bytes 6488068
  246.6 3.9 copy-start.10
  268.8 13.1 %all-to-all-start.2 = ((f32[32,1,768]{2,1,0:T(1,128)}), f32[32,1,768]{2,1,0:T(1,128)S(1)}, u32[]{:S(2)}, u32[]{:S(2)}) async-start(f32[32,1,768]{2,1,0:T(1,128)} %broadcast_in_dim.112), calls=%async_computation.2 | async-start | bytes 196608 | tf_op jit(solution)/shard_map/all_to_all | solution.py:139
  303.0 156.1 %all-to-all-start.3 = ((bf16[16,512,384]{2,0,1:T(8,128)(2,1)}), bf16[16,512,384]{2,0,1:T(8,128)(2,1)}, u32[]{:S(2)}, u32[]{:S(2)}) async-start(bf16[16,512,384]{2,0,1:T(8,128)(2,1)} %copy.111), calls=%async_computation.3 | async-start | bytes 12582912 | tf_op jit(solution)/shard_map/all_to_all | solution.py:152
  309.9 41.7 %collective-permute-start = (bf16[1,128,512]{2,1,0:T(8,128)(2,1)S(1)}, bf16[1,128,512]{2,1,0:T(8,128)(2,1)S(1)}, u32[]{:S(2)}, u32[]{:S(2)}) collective-permute-start(bf16[1,128,512]{2,1,0:T(8,128)(2,1)S(1)} %get-tuple-element.9), channel_id=1, source_target_pairs={{0,4},{4,8},{8,12},{12,16},{16,20},{20,24},{24,28},{1,5},{5,9},{9,... | collective-permute-start | bytes 393224 | tf_op jit(solution)/shard_map/ppermute | solution.py:68
  313.2 38.6 %collective-permute-start.1 = (bf16[1,128,512]{2,1,0:T(8,128)(2,1)S(1)}, bf16[1,128,512]{2,1,0:T(8,128)(2,1)S(1)}, u32[]{:S(2)}, u32[]{:S(2)}) collective-permute-start(bf16[1,128,512]{2,1,0:T(8,128)(2,1)S(1)} %get-tuple-element.10), channel_id=1, source_target_pairs={{4,0},{8,4},{12,8},{16,12},{20,16},{24,20},{28,24},{5,1},{9,5},{13... | collective-permute-start | bytes 393224 | tf_op jit(solution)/shard_map/ppermute | solution.py:70
  353.0 92.6 %collective-permute-start.2 = (bf16[66,1,512]{2,0,1:T(8,128)(2,1)S(1)}, bf16[66,1,512]{2,0,1:T(8,128)(2,1)S(1)}, u32[]{:S(2)}, u32[]{:S(2)}) collective-permute-start(bf16[66,1,512]{2,0,1:T(8,128)(2,1)S(1)} %get-tuple-element.7), channel_id=1, source_target_pairs={{0,1},{1,2},{2,3},{4,5},{5,6},{6,7},{8,9},{9,10},{10,11},{12,13},{... | collective-permute-start | bytes 202760 | tf_op jit(solution)/shard_map/ppermute | solution.py:68
  354.9 92.7 %collective-permute-start.3 = (bf16[66,1,512]{2,0,1:T(8,128)(2,1)S(1)}, bf16[66,1,512]{2,0,1:T(8,128)(2,1)S(1)}, u32[]{:S(2)}, u32[]{:S(2)}) collective-permute-start(bf16[66,1,512]{2,0,1:T(8,128)(2,1)S(1)} %get-tuple-element.8), channel_id=1, source_target_pairs={{1,0},{2,1},{3,2},{5,4},{6,5},{7,6},{9,8},{10,9},{11,10},{13,12},{... | collective-permute-start | bytes 202760 | tf_op jit(solution)/shard_map/ppermute | solution.py:70
  459.0 4.4 copy-start.11
  478.5 95.2 %all-to-all-start.4 = ((bf16[512,16,384]{2,1,0:T(8,128)(2,1)}), bf16[512,16,384]{2,1,0:T(8,128)(2,1)}, u32[]{:S(2)}, u32[]{:S(2)}) async-start(bf16[512,16,384]{2,1,0:T(8,128)(2,1)} %copy.114), calls=%async_computation.4 | async-start | bytes 12582912 | tf_op jit(solution)/shard_map/all_to_all | solution.py:154
  517.3 4.3 copy-start.2
  519.6 2.6 copy-start.8
  519.6 2.6 copy-start.13
  594.9 12.6 %copy-start.3 = (bf16[64,128,128]{2,0,1:T(8,128)(2,1)S(1)}, bf16[64,128,128]{2,0,1:T(8,128)(2,1)}, u32[]{:S(2)}) copy-start(bf16[64,128,128]{2,0,1:T(8,128)(2,1)} %slice_bitcast_fusion.2) | copy-start | bytes 6291460
  607.5 19.3 %copy-start.1 = (bf16[768,768]{1,0:T(8,128)(2,1)S(1)}, bf16[768,768]{1,0:T(8,128)(2,1)}, u32[]{:S(2)}) copy-start(bf16[768,768]{1,0:T(8,128)(2,1)} %param.22) | copy-start | bytes 3538948
where the time goes:
time: 632 us; the launch traced here: 627 us
  waiting for transfers between devices  258 us (41%)
  local copies, waits for them, and re-layouts  120 us (19%)
  matrix products  78.9 us (12%)
  blocking collectives  74.4 us (12%)
  other arithmetic  52.8 us (8%)
  starting transfers between devices  43.1 us (7%)
    all_to_all x1, waiting for transfers between devices, global_branch(): lines = lax.all_to_all(field, BOTH, split_axis=0, concat_axis=1, tiled=True)  137 us
    ppermute x2, waiting for transfers between devices, extended(): lax.ppermute(tail, axis, [(i, (i + 1) % count) for i in range(ends)])  118 us
    all_to_all x1, blocking collectives, global_branch(): lax.all_to_all(glob, 'row', split_axis=1, concat_axis=0, tiled=True)  74.4 us
    dot_general x5, matrix products, product(): return jnp.einsum(form, left, right, preferred_element_type=jnp.float32)  41.7 us
    conv_general_dilated x2, matrix products, conv(): lax.conv_general_dilated(padded[None], weight, (1, 1), 'VALID', dimension...  37.2 us
    conv_general_dilated x5, local copies, waits for them, and re-layouts, conv(): lax.conv_general_dilated(padded[None], weight, (1, 1), 'VALID', dimension...  23.4 us
    unnamed x29, local copies, waits for them, and re-layouts  13.2 us
    convert_element_type x1, local copies, waits for them, and re-layouts, body(): cross_out + spectral  12.8 us
  transfers between devices with their start and end apart: 8, of which 4 were waited for; matrix products, arithmetic and copies ran while one was open for 17% of the time, Pallas kernels for 0%

commit v1 on v0

--- a/solution.py
+++ b/solution.py
@@ -95,7 +95,23 @@
     height, width, ch = (glob.shape[0] * nrow, glob.shape[1] * ncol, glob.shape[2])
     bins = height // (2 * count)
     padded = -(-(width + 2) // 16) * 16
-    columns = lax.all_to_all(glob, "row", split_axis=1, concat_axis=0, tiled=True)
+    now, v_next = (lax.axis_size("row"), lax.axis_index("row"))
+    h_now = glob.shape[1] // now
+    left_arr = list(glob.shape)
+    left_arr[1] = h_now
+    b_next = left_arr[0]
+    left_arr[0] = b_next * now
+    columns = jnp.zeros(left_arr, glob.dtype)
+    for to_i in range(now):
+        arr_next = lax.dynamic_slice_in_dim(glob, (v_next ^ to_i) * h_now, h_now, axis=1)
+        if to_i:
+            entries = []
+            for dev in range(now):
+                entries.append((dev, dev ^ to_i))
+            arr_next = lax.ppermute(arr_next, "row", entries)
+        columns = lax.dynamic_update_slice_in_dim(
+            columns, arr_next, (v_next ^ to_i) * b_next, axis=0
+        )
     col_np = column_table(height)
     plain_np, packed_np, sign, upper, lower, scale_plain, scale_packed = width_tables(
         width_order(nrow, ncol, width), width, padded

time: 632 us -> 700 us (1.11); the launches traced: 627 us -> 687 us
  local copies, waits for them, and re-layouts: 120 us -> 240 us
  blocking collectives: 74.4 us -> 0 us
  starting transfers between devices: 43.1 us -> 53 us
    dynamic_update_slice x0 -> x8, local copies, waits for them, and re-layouts: none -> 95.9 us  [global_branch(): lax.dynamic_update_slice_in_dim(columns, arr_next, (v_next ^ to_i) * b_ne...]
    all_to_all x1 -> x0, blocking collectives: 74.4 us -> none  [global_branch(): lax.all_to_all(glob, 'row', split_axis=1, concat_axis=0, tiled=True)]
    ppermute x0 -> x7, waiting for transfers between devices: none -> 14.1 us  [global_branch(): arr_next = lax.ppermute(arr_next, 'row', entries)]
    ppermute x0 -> x7, local copies, waits for them, and re-layouts: none -> 11.9 us  [global_branch(): arr_next = lax.ppermute(arr_next, 'row', entries)]
    ppermute x2, waiting for transfers between devices: 118 us -> 107 us  [extended(): lax.ppermute(tail, axis, [(i, (i + 1) % count) for i in range(ends)])]
    ppermute x0 -> x7, starting transfers between devices: none -> 9.53 us  [global_branch(): arr_next = lax.ppermute(arr_next, 'row', entries)]
  transfers between devices with their start and end apart: 8 -> 15, of which waited for: 4 -> 5; matrix products, arithmetic and copies ran while one was open for 17% -> 31% of each run, Pallas kernels for 0% -> 0%
where the time goes in v1:
time: 700 us; the launch traced here: 687 us
  waiting for transfers between devices  260 us (37%)
  local copies, waits for them, and re-layouts  240 us (34%)
  matrix products  82.6 us (12%)
  starting transfers between devices  53 us (8%)
  other arithmetic  50.1 us (7%)
    all_to_all x1, waiting for transfers between devices, global_branch(): lines = lax.all_to_all(field, BOTH, split_axis=0, concat_axis=1, tiled=True)  137 us
    ppermute x2, waiting for transfers between devices, extended(): lax.ppermute(tail, axis, [(i, (i + 1) % count) for i in range(ends)])  107 us
    dynamic_update_slice x8, local copies, waits for them, and re-layouts, global_branch(): lax.dynamic_update_slice_in_dim(columns, arr_next, (v_next ^ to_i) * b_ne...  95.9 us
    dot_general x5, matrix products, product(): return jnp.einsum(form, left, right, preferred_element_type=jnp.float32)  45.7 us
    conv_general_dilated x2, matrix products, conv(): lax.conv_general_dilated(padded[None], weight, (1, 1), 'VALID', dimension...  36.9 us
    conv_general_dilated x5, local copies, waits for them, and re-layouts, conv(): lax.conv_general_dilated(padded[None], weight, (1, 1), 'VALID', dimension...  23.5 us
    ppermute x7, waiting for transfers between devices, global_branch(): arr_next = lax.ppermute(arr_next, 'row', entries)  14.1 us
  transfers between devices with their start and end apart: 15, of which 5 were waited for; matrix products, arithmetic and copies ran while one was open for 31% of the time, Pallas kernels for 0%

profile of v1, /device:TPU:11, one launch (start us, length us, event | category | flops | bytes accessed | tf_op | source)
XLA Modules:
  0.0 687.2 jit_solution(1228403910503429463)
XLA Ops:
  16.1 14.1 %collective-permute-done.5 = bf16[64,16,384]{2,1,0:T(8,128)(2,1)S(1)} collective-permute-done((bf16[64,16,384]{2,1,0:T(8,128)(2,1)S(1)}, bf16[64,16,384]{2,1,0:T(8,128)(2,1)S(1)}, u32[]{:S(2)}, u32[]{:S(2)}) %collective-permute-start.5) | collective-permute-done | bytes 786464 | tf_op jit(solution)/shard_map/ppermute | solution.py:111
  40.4 13.5 %dynamic_update_slice.24 = bf16[512,16,384]{0,2,1:T(8,128)(2,1)} dynamic-update-slice(bf16[512,16,384]{0,2,1:T(8,128)(2,1)} %broadcast_in_dim.109, bf16[64,16,384]{0,2,1:T(8,128)(2,1)S(1)} %copy.136, s32[]{:T(128)S(6)} %select_n.67, s32[]{:T(128)} %constant.20.clone.1, s32[]{:T(128)} %constant.20.clone.1) | dynamic-update-slice | bytes 1572868 | tf_op jit(solution)/shard_map/dynamic_update_slice | solution.py:112
  55.7 10.8 %dynamic_update_slice.25 = bf16[512,16,384]{0,2,1:T(8,128)(2,1)} dynamic-update-slice(bf16[512,16,384]{0,2,1:T(8,128)(2,1)} %dynamic_update_slice.24, bf16[64,16,384]{0,2,1:T(8,128)(2,1)S(1)} %copy.137, s32[]{:T(128)S(6)} %select_n.69, s32[]{:T(128)} %constant.20.clone.1, s32[]{:T(128)} %constant.20.clone.1) | dynamic-update-slice | bytes 1572868 | tf_op jit(solution)/shard_map/dynamic_update_slice | solution.py:112
  67.5 13.5 %dynamic_update_slice.26 = bf16[512,16,384]{0,2,1:T(8,128)(2,1)} dynamic-update-slice(bf16[512,16,384]{0,2,1:T(8,128)(2,1)} %dynamic_update_slice.25, bf16[64,16,384]{0,2,1:T(8,128)(2,1)S(1)} %copy.138, s32[]{:T(128)S(6)} %select_n.71, s32[]{:T(128)} %constant.20.clone.1, s32[]{:T(128)} %constant.20.clone.1) | dynamic-update-slice | bytes 1572868 | tf_op jit(solution)/shard_map/dynamic_update_slice | solution.py:112
  82.8 10.8 %dynamic_update_slice.27 = bf16[512,16,384]{0,2,1:T(8,128)(2,1)} dynamic-update-slice(bf16[512,16,384]{0,2,1:T(8,128)(2,1)} %dynamic_update_slice.26, bf16[64,16,384]{0,2,1:T(8,128)(2,1)S(1)} %copy.139, s32[]{:T(128)S(6)} %select_n.73, s32[]{:T(128)} %constant.20.clone.1, s32[]{:T(128)} %constant.20.clone.1) | dynamic-update-slice | bytes 1572868 | tf_op jit(solution)/shard_map/dynamic_update_slice | solution.py:112
  95.5 12.8 %dynamic_update_slice.28 = bf16[512,16,384]{0,2,1:T(8,128)(2,1)} dynamic-update-slice(bf16[512,16,384]{0,2,1:T(8,128)(2,1)} %dynamic_update_slice.27, bf16[64,16,384]{0,2,1:T(8,128)(2,1)S(1)} %copy.140, s32[]{:T(128)S(6)} %select_n.75, s32[]{:T(128)} %constant.20.clone.1, s32[]{:T(128)} %constant.20.clone.1) | dynamic-update-slice | bytes 1572868 | tf_op jit(solution)/shard_map/dynamic_update_slice | solution.py:112
  110.1 10.1 %dynamic_update_slice.29 = bf16[512,16,384]{0,2,1:T(8,128)(2,1)} dynamic-update-slice(bf16[512,16,384]{0,2,1:T(8,128)(2,1)} %dynamic_update_slice.28, bf16[64,16,384]{0,2,1:T(8,128)(2,1)S(1)} %copy.141, s32[]{:T(128)S(6)} %select_n.77, s32[]{:T(128)} %constant.20.clone.1, s32[]{:T(128)} %constant.20.clone.1) | dynamic-update-slice | bytes 1572868 | tf_op jit(solution)/shard_map/dynamic_update_slice | solution.py:112
  122.1 13.5 %dynamic_update_slice.30 = bf16[512,16,384]{0,2,1:T(8,128)(2,1)} dynamic-update-slice(bf16[512,16,384]{0,2,1:T(8,128)(2,1)} %dynamic_update_slice.29, bf16[64,16,384]{0,2,1:T(8,128)(2,1)S(1)} %copy.142, s32[]{:T(128)S(6)} %select_n.79, s32[]{:T(128)} %constant.20.clone.1, s32[]{:T(128)} %constant.20.clone.1) | dynamic-update-slice | bytes 1572868 | tf_op jit(solution)/shard_map/dynamic_update_slice | solution.py:112
  137.4 10.8 %dynamic_update_slice.31 = bf16[512,16,384]{0,2,1:T(8,128)(2,1)} dynamic-update-slice(bf16[512,16,384]{0,2,1:T(8,128)(2,1)} %dynamic_update_slice.30, bf16[64,16,384]{0,2,1:T(8,128)(2,1)S(1)} %copy.143, s32[]{:T(128)S(6)} %select_n.81, s32[]{:T(128)} %constant.20.clone.1, s32[]{:T(128)} %constant.20.clone.1) | dynamic-update-slice | bytes 1572868 | tf_op jit(solution)/shard_map/dynamic_update_slice | solution.py:112
  148.2 8.1 %convert_bitcast_fusion.2 = bf16[512,16,384]{0,2,1:T(8,128)(2,1)} fusion(bf16[512,16,384]{0,2,1:T(8,128)(2,1)} %dynamic_update_slice.31, bf16[512,512,1]{1,0,2:T(8,128)(2,1)S(1)} %copy-done.16), kind=kOutput, calls=%fused_computation.39 | convolution fusion | flops 3224371200 | bytes 13107200 | tf_op jit(solution)/shard_map/uh,hwc->uwc/dot_general | solution.py:89
  156.4 9.1 %copy.144 = bf16[512,16,384]{2,1,0:T(8,128)(2,1)} copy(bf16[512,16,384]{0,2,1:T(8,128)(2,1)} %convert_bitcast_fusion.2) | data formatting | bytes 12582912 | tf_op jit(solution)/shard_map/convert_element_type | solution.py:148
  172.2 137.3 %all-to-all-done = bf16[512,16,384]{2,1,0:T(8,128)(2,1)} async-done(((bf16[512,16,384]{2,1,0:T(8,128)(2,1)}), bf16[512,16,384]{2,1,0:T(8,128)(2,1)}, u32[]{:S(2)}, u32[]{:S(2)}) %all-to-all-start) | async-done | bytes 6291488 | tf_op jit(solution)/shard_map/all_to_all | solution.py:149
  313.4 9.8 %fusion.20 = bf16[8,1056,384]{2,1,0:T(8,128)(2,1)S(1)} fusion(bf16[8,1024,384]{2,1,0:T(8,128)(2,1)S(1)} %bitcast.63, pred[8]{0:T(512)(128)(4,1)S(1)} %compare_and_fusion, bf16[1056,1024]{1,0:T(8,128)(2,1)S(1)} %copy-done.13, bf16[1056,1024]{1,0:T(8,128)(2,1)S(1)} %copy-done.14), kind=kOutput, calls=%fused_computation.28 | convolution fusion | flops 6655672320 | bytes 17104904 | tf_op jit(solution)/shard_map/bmk,bkc->bmc/dot_general | solution.py:89
  344.4 14.6 %subtract_convert_fusion = bf16[8,1024,384]{2,1,0:T(8,128)(2,1)S(1)} fusion(bf16[8,528,384]{2,1,0:T(8,128)(2,1)} %get-tuple-element.12, bf16[8,528,384]{2,1,0:T(8,128)(2,1)} %get-tuple-element.11, pred[8]{0:T(512)(128)(4,1)S(1)} %compare_and_fusion, bf16[1056,1024]{1,0:T(8,128)(2,1)S(1)} %copy-done.13, bf16[1056,1024]{1,0:T(8,128)(2,1)} %constant.104, ...), kind=kOutput, calls=%fused_computation.13 | convolution fusion | flops 6681133056 | bytes 17173512 | tf_op jit(solution)/shard_map/bkm,bkc->bmc/dot_general | solution.py:89
  377.9 11.5 %copy.128 = bf16[64,128,512]{2,0,1:T(8,128)(2,1)} copy(bf16[64,128,512]{2,1,0:T(8,128)(2,1)} %param.19) | data formatting | bytes 16777216 | tf_op args[0]
  389.4 24.7 %collective-permute-done = bf16[1,128,512]{2,1,0:T(8,128)(2,1)S(1)} collective-permute-done((bf16[1,128,512]{2,1,0:T(8,128)(2,1)S(1)}, bf16[1,128,512]{2,1,0:T(8,128)(2,1)S(1)}, u32[]{:S(2)}, u32[]{:S(2)}) %collective-permute-start) | collective-permute-done | bytes 131104 | tf_op jit(solution)/shard_map/ppermute | solution.py:68
  417.4 8.5 %collective-permute-start.3 = (bf16[66,1,512]{2,0,1:T(8,128)(2,1)S(1)}, bf16[66,1,512]{2,0,1:T(8,128)(2,1)S(1)}, u32[]{:S(2)}, u32[]{:S(2)}) collective-permute-start(bf16[66,1,512]{2,0,1:T(8,128)(2,1)S(1)} %get-tuple-element.8), channel_id=1, source_target_pairs={{1,0},{2,1},{3,2},{5,4},{6,5},{7,6},{9,8},{10,9},{11,10},{13,12},{... | collective-permute-start | bytes 202760 | tf_op jit(solution)/shard_map/ppermute | solution.py:70
  425.9 82.1 %collective-permute-done.2 = bf16[66,1,512]{2,0,1:T(8,128)(2,1)S(1)} collective-permute-done((bf16[66,1,512]{2,0,1:T(8,128)(2,1)S(1)}, bf16[66,1,512]{2,0,1:T(8,128)(2,1)S(1)}, u32[]{:S(2)}, u32[]{:S(2)}) %collective-permute-start.2) | collective-permute-done | bytes 67616 | tf_op jit(solution)/shard_map/ppermute | solution.py:68
  510.0 8.7 %fusion.68 = bf16[66,1,130,512]{3,0,2,1:T(8,128)(2,1)} fusion(bf16[66,1,512]{2,0,1:T(8,128)(2,1)S(1)} %collective-permute-done.3, bf16[1,128,512]{2,0,1:T(2,128)(2,1)S(1)} %copy.129, bf16[64,128,512]{2,0,1:T(8,128)(2,1)S(1)} %copy-done.2, bf16[1,128,512]{2,0,1:T(2,128)(2,1)S(1)} %copy.127, bf16[66,1,512]{2,0,1:T(8,128)(2,1)S(1)} %collective-permute-done.2), kind=kLoop, calls=%fused_computation.82 | loop fusion | flops 43929600 | bytes 17571840 | tf_op jit(solution)/shard_map/broadcast_in_dim | solution.py:79
  529.1 9.1 %copy.150 = bf16[512,16,384]{2,1,0:T(8,128)(2,1)} copy(bf16[512,16,384]{0,2,1:T(8,128)(2,1)} %convert_bitcast_fusion.1) | data formatting | bytes 12582912 | tf_op jit(solution)/shard_map/convert_element_type | solution.py:169
  538.2 8.8 %all-to-all-start.3 = ((bf16[512,16,384]{2,1,0:T(8,128)(2,1)}), bf16[512,16,384]{2,1,0:T(8,128)(2,1)}, u32[]{:S(2)}, u32[]{:S(2)}) async-start(bf16[512,16,384]{2,1,0:T(8,128)(2,1)} %copy.150), calls=%async_computation.3 | async-start | bytes 12582912 | tf_op jit(solution)/shard_map/all_to_all | solution.py:170
  547.0 11.5 %pad_maximum_fusion = bf16[66,130,512]{2,0,1:T(8,128)(2,1)} fusion(bf16[66,1,512]{2,0,1:T(8,128)(2,1)S(1)} %collective-permute-done.3, bf16[1,128,512]{2,0,1:T(2,128)(2,1)S(1)} %copy.129, bf16[64,128,512]{2,0,1:T(8,128)(2,1)} %copy.128, bf16[1,128,512]{2,0,1:T(2,128)(2,1)S(1)} %copy.127, bf16[66,1,512]{2,0,1:T(8,128)(2,1)S(1)} %collective-permute-done.2), kind=kLoop, calls=%fused_computation.21 | loop fusion | flops 43929600 | bytes 17571840 | tf_op jit(solution)/shard_map/concatenate | solution.py:66
  558.5 8.2 %pad = bf16[66,1,136,512]{3,0,2,1:T(8,128)(2,1)} pad(bf16[66,1,130,512]{3,0,2,1:T(8,128)(2,1)} %fusion.68, bf16[]{:T(256)} %constant.21.clone.1), padding=0_0x0_0x0_6x0_0 | pad | bytes 17977346 | tf_op jit(solution)/shard_map/broadcast_in_dim | solution.py:79
  566.7 10.6 %copy.131 = bf16[66,1,8,17,512]{4,2,3,0,1:T(8,128)(2,1)} copy(bf16[66,1,8,17,512]{4,0,3,2,1:T(8,128)(2,1)} %bitcast.58) | data formatting | bytes 18382848 | tf_op jit(solution)/shard_map/conv_general_dilated | solution.py:78
  582.2 21.4 %select_convert_fusion = bf16[64,8,17,128]{3,1,2,0:T(8,128)(2,1)S(1)} fusion(pred[8,17]{0,1:T(8,128)(4,1)S(1)} %copy-done.17, bf16[3,3,512,128]{3,2,1,0:T(8,128)(2,1)S(1)} %copy-done.12, bf16[66,1,7,2,512]{4,2,3,0,1:T(8,128)(2,1)S(1)} %slice.76, bf16[66,1,8,17,512]{4,2,3,0,1:T(8,128)(2,1)S(1)} %copy-done.3), kind=kOutput, calls=%fused_computation.43 | convolution fusion | flops 10300702720 | bytes 13545608 | tf_op jit(solution)/shard_map/conv_general_dilated | solution.py:78
  604.1 15.6 %convolution_select_fusion = f32[64,8,17,384]{3,1,2,0:T(8,128)} fusion(bf16[3,3,128,384]{3,2,1,0:T(8,128)(2,1)} %param.21, pred[8,17]{0,1:T(8,128)(4,1)S(1)} %copy-done.17, bf16[66,1,7,2,128]{4,2,3,0,1:T(8,128)(2,1)S(1)} %slice.79, bf16[66,1,8,17,128]{4,2,3,0,1:T(8,128)(2,1)S(1)} %copy.134), kind=kOutput, calls=%fused_computation.22 | convolution fusion | flops 7711789056 | bytes 16788616 | tf_op jit(solution)/shard_map/conv_general_dilated | solution.py:78
  619.7 12.2 %copy.135 = f32[64,8,17,384]{3,0,2,1:T(8,128)} copy(f32[64,8,17,384]{3,1,2,0:T(8,128)} %convolution_select_fusion) | data formatting | bytes 26738688 | tf_op jit(solution)/shard_map/conv_general_dilated | solution.py:78
  633.4 8.4 %convert_bitcast_fusion = f32[64,8,16,384]{3,2,0,1:T(8,128)} fusion(bf16[8,64,16,384]{3,2,1,0:T(8,128)(2,1)} %bitcast.26), kind=kLoop, calls=%fused_computation.12 | loop fusion | flops 3145728 | bytes 18874368 | tf_op jit(solution)/shard_map/convert_element_type | solution.py:180
  641.8 12.8 %copy.151 = f32[64,8,16,384]{3,0,2,1:T(8,128)} copy(f32[64,8,16,384]{3,2,0,1:T(8,128)} %convert_bitcast_fusion) | data formatting | bytes 25165824 | tf_op jit(solution)/shard_map/convert_element_type | solution.py:180
  654.7 12.7 %fusion.8 = bf16[64,128,384]{2,0,1:T(8,128)(2,1)} fusion(f32[64,1,136,384]{3,0,2,1:T(8,128)} %bitcast.57, f32[64,8,16,384]{3,0,2,1:T(8,128)} %copy.151), kind=kLoop, calls=%fused_computation.11 | loop fusion | flops 6291456 | bytes 31457280 | tf_op jit(solution)/shard_map/convert_element_type | solution.py:180
  667.4 7.8 %pad_maximum_fusion.1 = bf16[64,128,512]{2,0,1:T(8,128)(2,1)} fusion(bf16[64,128,384]{2,0,1:T(8,128)(2,1)} %fusion.8, bf16[64,128,128]{2,0,1:T(8,128)(2,1)S(1)} %copy-done.4), kind=kLoop, calls=%fused_computation.27 | loop fusion | flops 16777216 | bytes 16777216 | tf_op jit(solution)/shard_map/concatenate | solution.py:179
  675.1 11.5 %copy.152 = bf16[64,128,512]{2,1,0:T(8,128)(2,1)} copy(bf16[64,128,512]{2,0,1:T(8,128)(2,1)} %pad_maximum_fusion.1) | data formatting | bytes 16777216 | tf_op jit(solution)/shard_map/concatenate | solution.py:179
  (97 shorter events, 111.3 us)
Async XLA Ops:
  0.0 323.8 %copy-start = (bf16[768,768]{1,0:T(8,128)(2,1)S(1)}, bf16[768,768]{1,0:T(8,128)(2,1)}, u32[]{:S(2)}) copy-start(bf16[768,768]{1,0:T(8,128)(2,1)} %param.22) | copy-start | bytes 3538948
  11.6 18.5 %collective-permute-start.5 = (bf16[64,16,384]{2,1,0:T(8,128)(2,1)S(1)}, bf16[64,16,384]{2,1,0:T(8,128)(2,1)S(1)}, u32[]{:S(2)}, u32[]{:S(2)}) collective-permute-start(bf16[64,16,384]{2,1,0:T(8,128)(2,1)S(1)} %get-tuple-element.20), channel_id=1, source_target_pairs={{0,8},{4,12},{8,0},{12,4},{16,24},{20,28},{24,16},{28,20},{1,9},{5... | collective-permute-start | bytes 2359304 | tf_op jit(solution)/shard_map/ppermute | solution.py:111
  11.9 19.5 %collective-permute-start.4 = (bf16[64,16,384]{2,1,0:T(8,128)(2,1)S(1)}, bf16[64,16,384]{2,1,0:T(8,128)(2,1)S(1)}, u32[]{:S(2)}, u32[]{:S(2)}) collective-permute-start(bf16[64,16,384]{2,1,0:T(8,128)(2,1)S(1)} %get-tuple-element.21), channel_id=1, source_target_pairs={{0,4},{4,0},{8,12},{12,8},{16,20},{20,16},{24,28},{28,24},{1,5},{5... | collective-permute-start | bytes 2359304 | tf_op jit(solution)/shard_map/ppermute | solution.py:111
  12.8 68.2 %collective-permute-start.6 = (bf16[64,16,384]{2,1,0:T(8,128)(2,1)}, bf16[64,16,384]{2,1,0:T(8,128)(2,1)}, u32[]{:S(2)}, u32[]{:S(2)}) collective-permute-start(bf16[64,16,384]{2,1,0:T(8,128)(2,1)} %get-tuple-element.19), channel_id=1, source_target_pairs={{0,12},{4,8},{8,4},{12,0},{16,28},{20,24},{24,20},{28,16},{1,13},{... | collective-permute-start | bytes 2359304 | tf_op jit(solution)/shard_map/ppermute | solution.py:111
  13.9 79.7 %collective-permute-start.7 = (bf16[64,16,384]{2,1,0:T(8,128)(2,1)}, bf16[64,16,384]{2,1,0:T(8,128)(2,1)}, u32[]{:S(2)}, u32[]{:S(2)}) collective-permute-start(bf16[64,16,384]{2,1,0:T(8,128)(2,1)} %get-tuple-element.18), channel_id=1, source_target_pairs={{0,16},{4,20},{8,24},{12,28},{16,0},{20,4},{24,8},{28,12},{1,17},{... | collective-permute-start | bytes 2359304 | tf_op jit(solution)/shard_map/ppermute | solution.py:111
  15.2 93.1 %collective-permute-start.8 = (bf16[64,16,384]{2,1,0:T(8,128)(2,1)}, bf16[64,16,384]{2,1,0:T(8,128)(2,1)}, u32[]{:S(2)}, u32[]{:S(2)}) collective-permute-start(bf16[64,16,384]{2,1,0:T(8,128)(2,1)} %get-tuple-element.17), channel_id=1, source_target_pairs={{0,20},{4,16},{8,28},{12,24},{16,4},{20,0},{24,12},{28,8},{1,21},{... | collective-permute-start | bytes 2359304 | tf_op jit(solution)/shard_map/ppermute | solution.py:111
  30.1 1.2 copy-start.5
  30.2 90.1 %collective-permute-start.9 = (bf16[64,16,384]{2,1,0:T(8,128)(2,1)}, bf16[64,16,384]{2,1,0:T(8,128)(2,1)}, u32[]{:S(2)}, u32[]{:S(2)}) collective-permute-start(bf16[64,16,384]{2,1,0:T(8,128)(2,1)} %get-tuple-element.16), channel_id=1, source_target_pairs={{0,24},{4,28},{8,16},{12,20},{16,8},{20,12},{24,0},{28,4},{1,25},{... | collective-permute-start | bytes 2359304 | tf_op jit(solution)/shard_map/ppermute | solution.py:111
  32.2 103.4 %collective-permute-start.10 = (bf16[64,16,384]{2,1,0:T(8,128)(2,1)}, bf16[64,16,384]{2,1,0:T(8,128)(2,1)}, u32[]{:S(2)}, u32[]{:S(2)}) collective-permute-start(bf16[64,16,384]{2,1,0:T(8,128)(2,1)} %get-tuple-element.15), channel_id=1, source_target_pairs={{0,28},{4,24},{8,20},{12,16},{16,12},{20,8},{24,4},{28,0},{1,29},{... | collective-permute-start | bytes 2359304 | tf_op jit(solution)/shard_map/ppermute | solution.py:111
  37.1 29.5 %copy-start.6 = (bf16[64,16,384]{2,1,0:T(8,128)(2,1)S(1)}, bf16[64,16,384]{2,1,0:T(8,128)(2,1)}, u32[]{:S(2)}) copy-start(bf16[64,16,384]{2,1,0:T(8,128)(2,1)} %copy-done.5) | copy-start | bytes 2359300
  110.1 38.1 %copy-start.16 = (bf16[512,512,1]{1,0,2:T(8,128)(2,1)S(1)}, bf16[512,512,1]{1,0,2:T(8,128)(2,1)}, u32[]{:S(2)}) copy-start(bf16[512,512,1]{1,0,2:T(8,128)(2,1)} %constant.117) | copy-start | bytes 1572868
  165.4 6.6 copy-start.10
  165.4 6.6 copy-start.11
  165.4 6.6 copy-start.8
  165.4 6.6 copy-start.9
  165.5 144.0 %all-to-all-start = ((bf16[512,16,384]{2,1,0:T(8,128)(2,1)}), bf16[512,16,384]{2,1,0:T(8,128)(2,1)}, u32[]{:S(2)}, u32[]{:S(2)}) async-start(bf16[512,16,384]{2,1,0:T(8,128)(2,1)} %copy.144), calls=%async_computation | async-start | bytes 12582912 | tf_op jit(solution)/shard_map/all_to_all | solution.py:149
  172.0 141.4 %copy-start.13 = (bf16[1056,1024]{1,0:T(8,128)(2,1)S(1)}, bf16[1056,1024]{1,0:T(8,128)(2,1)}, u32[]{:S(2)}) copy-start(bf16[1056,1024]{1,0:T(8,128)(2,1)} %constant.113) | copy-start | bytes 6488068
  309.4 3.9 copy-start.14
  331.6 12.7 %all-to-all-start.1 = ((f32[32,1,768]{2,1,0:T(1,128)}), f32[32,1,768]{2,1,0:T(1,128)S(1)}, u32[]{:S(2)}, u32[]{:S(2)}) async-start(f32[32,1,768]{2,1,0:T(1,128)} %broadcast_in_dim.116), calls=%async_computation.1 | async-start | bytes 196608 | tf_op jit(solution)/shard_map/all_to_all | solution.py:155
  365.4 153.2 %all-to-all-start.2 = ((bf16[16,512,384]{2,0,1:T(8,128)(2,1)}), bf16[16,512,384]{2,0,1:T(8,128)(2,1)}, u32[]{:S(2)}, u32[]{:S(2)}) async-start(bf16[16,512,384]{2,0,1:T(8,128)(2,1)} %copy.147), calls=%async_computation.2 | async-start | bytes 12582912 | tf_op jit(solution)/shard_map/all_to_all | solution.py:168
  372.3 41.7 %collective-permute-start = (bf16[1,128,512]{2,1,0:T(8,128)(2,1)S(1)}, bf16[1,128,512]{2,1,0:T(8,128)(2,1)S(1)}, u32[]{:S(2)}, u32[]{:S(2)}) collective-permute-start(bf16[1,128,512]{2,1,0:T(8,128)(2,1)S(1)} %get-tuple-element.9), channel_id=1, source_target_pairs={{0,4},{4,8},{8,12},{12,16},{16,20},{20,24},{24,28},{1,5},{5,9},{9,... | collective-permute-start | bytes 393224 | tf_op jit(solution)/shard_map/ppermute | solution.py:68
  375.7 38.6 %collective-permute-start.1 = (bf16[1,128,512]{2,1,0:T(8,128)(2,1)S(1)}, bf16[1,128,512]{2,1,0:T(8,128)(2,1)S(1)}, u32[]{:S(2)}, u32[]{:S(2)}) collective-permute-start(bf16[1,128,512]{2,1,0:T(8,128)(2,1)S(1)} %get-tuple-element.10), channel_id=1, source_target_pairs={{4,0},{8,4},{12,8},{16,12},{20,16},{24,20},{28,24},{5,1},{9,5},{13... | collective-permute-start | bytes 393224 | tf_op jit(solution)/shard_map/ppermute | solution.py:70
  389.4 120.7 %copy-start.2 = (bf16[64,128,512]{2,0,1:T(8,128)(2,1)S(1)}, bf16[64,128,512]{2,0,1:T(8,128)(2,1)}, u32[]{:S(2)}) copy-start(bf16[64,128,512]{2,0,1:T(8,128)(2,1)} %copy.128) | copy-start | bytes 25165828
  415.4 92.6 %collective-permute-start.2 = (bf16[66,1,512]{2,0,1:T(8,128)(2,1)S(1)}, bf16[66,1,512]{2,0,1:T(8,128)(2,1)S(1)}, u32[]{:S(2)}, u32[]{:S(2)}) collective-permute-start(bf16[66,1,512]{2,0,1:T(8,128)(2,1)S(1)} %get-tuple-element.7), channel_id=1, source_target_pairs={{0,1},{1,2},{2,3},{4,5},{5,6},{6,7},{8,9},{9,10},{10,11},{12,13},{... | collective-permute-start | bytes 202760 | tf_op jit(solution)/shard_map/ppermute | solution.py:68
  417.4 92.7 %collective-permute-start.3 = (bf16[66,1,512]{2,0,1:T(8,128)(2,1)S(1)}, bf16[66,1,512]{2,0,1:T(8,128)(2,1)S(1)}, u32[]{:S(2)}, u32[]{:S(2)}) collective-permute-start(bf16[66,1,512]{2,0,1:T(8,128)(2,1)S(1)} %get-tuple-element.8), channel_id=1, source_target_pairs={{1,0},{2,1},{3,2},{5,4},{6,5},{7,6},{9,8},{10,9},{11,10},{13,12},{... | collective-permute-start | bytes 202760 | tf_op jit(solution)/shard_map/ppermute | solution.py:70
  518.7 4.4 copy-start.15
  538.2 95.2 %all-to-all-start.3 = ((bf16[512,16,384]{2,1,0:T(8,128)(2,1)}), bf16[512,16,384]{2,1,0:T(8,128)(2,1)}, u32[]{:S(2)}, u32[]{:S(2)}) async-start(bf16[512,16,384]{2,1,0:T(8,128)(2,1)} %copy.150), calls=%async_computation.3 | async-start | bytes 12582912 | tf_op jit(solution)/shard_map/all_to_all | solution.py:170
  577.3 4.3 copy-start.3
  579.6 2.6 copy-start.12
  579.6 2.6 copy-start.17
  654.7 12.7 %copy-start.4 = (bf16[64,128,128]{2,0,1:T(8,128)(2,1)S(1)}, bf16[64,128,128]{2,0,1:T(8,128)(2,1)}, u32[]{:S(2)}) copy-start(bf16[64,128,128]{2,0,1:T(8,128)(2,1)} %slice_bitcast_fusion.2) | copy-start | bytes 6291460
  667.4 19.3 %copy-start.1 = (bf16[768,768]{1,0:T(8,128)(2,1)S(1)}, bf16[768,768]{1,0:T(8,128)(2,1)}, u32[]{:S(2)}) copy-start(bf16[768,768]{1,0:T(8,128)(2,1)} %param.22) | copy-start | bytes 3538948
  (1 other events, 0.9 us)
